TPU v7x, 32 devices: a whole 2x2x4 slice. The times are simulated.
32 devices in a mesh: dp: 16 (over z, y, x), mp: 2 (over core).
Axes of the slice: x: 2, y: 2, z: 4, core: 2. Of those that a mesh axis runs over, the one named last changes fastest.
Arguments:
- inputs: bfloat16 [32768, 4096], P('dp', 'mp'), may hold values from -6 to 6
- cotangents: bfloat16 [32768, 4096], P('dp', 'mp'), may hold values from -6 to 6
- loss_token_mask: int32 [32768], P('dp'), may hold values 0 or 1
- adapter_down_weight: bfloat16 [128, 4096], P(None, 'mp'), may hold values from -0.09375 to 0.09375
- adapter_up_weight: bfloat16 [4096, 128], P('mp'), may hold values from -0.5 to 0.5
- width_projection: bfloat16 [2, 4096, 256], P(None, 'mp'), may hold values from -0.09375 to 0.09375
- rank_projection: bfloat16 [2, 128, 16], replicated, may hold values from -0.5 to 0.5
- targets: float32 [64, 8192], P(None, ('dp', 'mp')), may hold values from -500 to 500
Outputs:
- scores: float32 [128, 64], P('dp')
All inputs are finite; a program needn't handle non-finite values. No bound on the sum of `loss_token_mask` on one device may be relied on, other than what follows from the above.
Results may differ from a plain program's by a relative error of at most 0.0003.
Values sent between devices are 32-bit elements; how exact they have to be, the bound alone decides.
A program may use at most 64 MiB of HBM per device.

v0:
```python
import math
import jax
import jax.numpy as jnp
from jax import lax
from jax.sharding import PartitionSpec as P

SEQ = 256
KP = 256
KQ = 16
FEAT = 8192
adapter_scale = 4.0
epsilon = 1e-06


def on_device(
    inputs,
    cotangents,
    loss_token_mask,
    adapter_down_weight,
    adapter_up_weight,
    width_projection,
    rank_projection,
    targets,
):
    samples = inputs.shape[0] // SEQ
    masked_gradient = cotangents * loss_token_mask.astype(jnp.bfloat16)[:, None]
    cols_first = rank_projection[0].astype(jnp.float32)
    cols_second = rank_projection[1].astype(jnp.float32)
    down_partial_gradient = jnp.dot(
        inputs, adapter_down_weight.T, preferred_element_type=jnp.float32
    )
    up_partial_gradient = jnp.dot(
        masked_gradient, adapter_up_weight, preferred_element_type=jnp.float32
    )
    down_rank_product, up_rank_product = lax.psum(
        (down_partial_gradient, up_partial_gradient), "mp"
    )
    compact_up_gradient = jnp.dot(up_rank_product, cols_first, precision=lax.Precision.HIGHEST)
    compact_down_gradient = jnp.dot(down_rank_product, cols_second, precision=lax.Precision.HIGHEST)
    projected_activations = jnp.dot(
        inputs, width_projection[0], preferred_element_type=jnp.float32
    ).reshape(samples, SEQ, KP)
    projected_masked_gradient = jnp.dot(
        masked_gradient, width_projection[1], preferred_element_type=jnp.float32
    ).reshape(samples, SEQ, KP)
    first_matrix = adapter_scale * jnp.einsum(
        "stk,stq->skq",
        projected_activations,
        compact_up_gradient.reshape(samples, SEQ, KQ),
        precision=lax.Precision.HIGHEST,
    )
    second_matrix = adapter_scale * jnp.einsum(
        "stk,stq->skq",
        projected_masked_gradient,
        compact_down_gradient.reshape(samples, SEQ, KQ),
        precision=lax.Precision.HIGHEST,
    )
    partial_value = jnp.concatenate(
        [first_matrix.reshape(samples, KP * KQ), second_matrix.reshape(samples, KP * KQ)], axis=1
    )
    features = lax.psum(partial_value, "mp")
    every_target = lax.all_gather(targets, ("dp", "mp"), axis=1, tiled=True)
    inner = jnp.dot(features, every_target.T, precision=lax.Precision.HIGHEST)
    sample_squares = jnp.sum(features * features, axis=1)
    target_squares = jnp.sum(every_target * every_target, axis=1)
    sample_rms = jnp.sqrt(sample_squares / FEAT + epsilon)
    target_rms = jnp.sqrt(target_squares / FEAT + epsilon)
    return inner / (math.sqrt(FEAT) * sample_rms[:, None] * target_rms[None, :])


def solution(mesh):
    in_specs = (
        P("dp", "mp"),
        P("dp", "mp"),
        P("dp"),
        P(None, "mp"),
        P("mp", None),
        P(None, "mp", None),
        P(),
        P(None, ("dp", "mp")),
    )
    out_specs = P("dp", None)
    return jax.shard_map(
        on_device, mesh=mesh, in_specs=in_specs, out_specs=out_specs, check_vma=False
    )
```

profile of v0, /device:TPU:0, one launch (start us, length us, event | category | flops | bytes accessed | tf_op | source)
XLA Modules:
  0.0 130.8 jit_solution(16499203396642434931)
XLA Ops:
  7.4 0.0 copy-start
  7.4 0.0 all-reduce.6.cloned.1.call-start
  7.4 0.8 convert_element_type.2
  8.1 7.2 %broadcast_multiply_fusion = bf16[2048,2048]{1,0:T(8,128)(2,1)} fusion(bf16[2048,2048]{1,0:T(8,128)(2,1)} %param.9, bf16[2048]{0:T(1024)(128)(2,1)S(1)} %convert_element_type.2), kind=kLoop, calls=%fused_computation | loop fusion | flops 4194304 | bytes 16781312 | tf_op jit(solution)/shard_map/mul | solution.py:26
  15.4 0.0 copy-done
  15.4 0.0 copy-start.1
  15.4 0.0 copy-start.7
  15.4 6.9 %fusion.13 = f32[2048,128]{1,0:T(8,128)} fusion(bf16[2048,2048]{1,0:T(8,128)(2,1)} %param.8, bf16[128,2048]{1,0:T(8,128)(2,1)S(1)} %copy-done), kind=kOutput, calls=%fused_computation.22 | convolution fusion | flops 1073741824 | bytes 9961472 | tf_op jit(solution)/shard_map/dot_general | solution.py:29
  22.2 0.0 copy-done.1
  22.2 0.0 copy-done.7
  22.3 3.4 %fusion.12 = f32[2048,128]{1,0:T(8,128)} fusion(bf16[2048,2048]{1,0:T(8,128)(2,1)S(1)} %copy-done.1, bf16[2048,128]{1,0:T(8,128)(2,1)S(1)} %copy-done.7), kind=kOutput, calls=%fused_computation.21 | convolution fusion | flops 1073741824 | bytes 9961472 | tf_op jit(solution)/shard_map/dot_general | solution.py:32
  25.7 0.0 all-reduce.6.cloned.1.call-update
  25.7 0.2 all-reduce.4.cloned.1.call-start
  25.9 0.0 copy-start.6
  25.9 6.1 %fusion = f32[8,256,256]{2,1,0:T(8,128)S(1)} fusion(bf16[8,256,2048]{2,1,0:T(8,128)(2,1)} %bitcast.34, bf16[2,2048,256]{2,1,0:T(8,128)(2,1)} %param.13), kind=kOutput, calls=%fused_computation.5 | convolution fusion | flops 2147483648 | bytes 11534336 | tf_op jit(solution)/shard_map/dot_general | solution.py:43
  32.0 0.0 copy-done.6
  32.1 0.0 copy-start.5
  32.1 7.8 %fusion.2 = f32[8,256,256]{2,1,0:T(8,128)} fusion(bf16[8,256,2048]{2,1,0:T(8,128)(2,1)} %bitcast.37, bf16[2,2048,256]{2,1,0:T(8,128)(2,1)S(1)} %copy-done.6), kind=kOutput, calls=%fused_computation.7 | convolution fusion | flops 2147483648 | bytes 11534336 | tf_op jit(solution)/shard_map/dot_general | solution.py:40
  39.9 10.0 %all-reduce.6.cloned.1.call-done = (f32[8,256,128]{2,1,0:T(8,128)}, f32[8,256,128]{2,1,0:T(8,128)}) async-done(((f32[8,256,128]{2,1,0:T(8,128)}, f32[8,256,128]{2,1,0:T(8,128)}), (f32[8,256,128]{2,1,0:T(8,128)}, f32[8,256,128]{2,1,0:T(8,128)})) %all-reduce.6.cloned.1.call-update) | async-done | bytes 2097168 | tf_op jit(solution)/shard_map/psum | solution.py:35
  49.8 0.0 copy-done.5
  49.8 1.8 %fusion.6 = f32[8,256,16]{1,2,0:T(8,128)S(1)} fusion(f32[8,256,128]{2,1,0:T(8,128)} %get-tuple-element.5, bf16[2,128,16]{1,2,0:T(8,128)(2,1)S(1)} %copy-done.5), kind=kOutput, calls=%fused_computation.13 | convolution fusion | flops 50331648 | bytes 1183744 | tf_op jit(solution)/shard_map/dot_general | solution.py:39
  51.6 1.2 convolution_multiply_fusion
  52.8 0.0 copy-start.4
  52.9 0.3 copy.10
  53.2 0.6 reshape.28
  53.8 0.3 copy-done.4
  54.1 0.6 fusion.8
  54.7 2.8 %convolution_multiply_fusion.1 = f32[8,256,16]{1,2,0:T(8,128)S(1)} fusion(f32[8,256,256]{2,1,0:T(8,128)} %fusion.2, f32[8,256,16]{1,2,0:T(8,128)S(1)} %fusion.8), kind=kOutput, calls=%fused_computation.3 | convolution fusion | flops 100696064 | bytes 2359296 | tf_op jit(solution)/shard_map/stk,stq->skq/dot_general | solution.py:46
  57.5 0.3 copy.9
  57.8 0.6 reshape.27
  58.4 0.7 pad_maximum_fusion
  59.2 0.0 all-reduce.4.cloned.1.call-update
  59.2 0.0 all-gather.2.cloned.1.call-start
  59.2 0.5 all-gather.2.cloned.1.call-update
  59.8 19.0 %all-reduce.4.cloned.1.call-done = f32[8,8192]{1,0:T(8,128)} async-done(((f32[8,8192]{1,0:T(8,128)}), f32[8,8192]{1,0:T(8,128)}) %all-reduce.4.cloned.1.call-update) | async-done | bytes 262160 | tf_op jit(solution)/shard_map/psum | solution.py:61
  78.8 0.0 copy-start.3
  78.8 1.2 multiply_reduce_fusion.1
  80.0 38.8 %all-gather.2.cloned.1.call-done = f32[64,8192]{1,0:T(8,128)} async-done(((f32[64,256]{1,0:T(8,128)}), f32[64,8192]{1,0:T(8,128)}) %all-gather.2.cloned.1.call-update) | async-done | bytes 2097168 | tf_op jit(solution)/shard_map/all_gather | solution.py:62
  118.8 0.0 copy-start.2
  118.8 2.0 %multiply_reduce_fusion = f32[64]{0:T(128)S(1)} fusion(f32[64,8192]{1,0:T(8,128)} %all-gather.2.cloned.1.call-done), kind=kLoop, calls=%fused_computation.1 | loop fusion | flops 1048512 | bytes 2097408 | tf_op jit(solution)/shard_map/reduce_sum | solution.py:65
  120.8 0.0 copy-done.3
  120.8 0.2 copy-done.2
  121.0 2.3 %convolution_divide_fusion = f32[8,64]{1,0:T(8,128)} fusion(f32[8,8192]{1,0:T(8,128)S(1)} %copy-done.3, f32[64,8192]{1,0:T(8,128)S(1)} %copy-done.2, f32[64]{0:T(128)S(1)} %add_sqrt_fusion, f32[8]{0:T(128)S(1)} %sqrt_multiply_fusion), kind=kOutput, calls=%fused_computation.4 | convolution fusion | flops 50332672 | bytes 2361632 | tf_op jit(solution)/shard_map/dot_general | solution.py:63
  (2 shorter events, 0.0 us)
Async XLA Ops:
  7.4 8.0 %copy-start = (bf16[128,2048]{1,0:T(8,128)(2,1)S(1)}, bf16[128,2048]{1,0:T(8,128)(2,1)}, u32[]{:S(2)}) copy-start(bf16[128,2048]{1,0:T(8,128)(2,1)} %param.11) | copy-start | bytes 1572868
  7.4 42.5 %all-reduce.6.cloned.1.call-start = ((), (), s32[]{:S(2)}) async-start(), calls=%async_computation.2 | async-start | bytes 4194304 | tf_op jit(solution)/shard_map/psum | solution.py:35
  15.4 6.9 %copy-start.1 = (bf16[2048,2048]{1,0:T(8,128)(2,1)S(1)}, bf16[2048,2048]{1,0:T(8,128)(2,1)}, u32[]{:S(2)}) copy-start(bf16[2048,2048]{1,0:T(8,128)(2,1)} %broadcast_multiply_fusion) | copy-start | bytes 25165828
  15.4 6.9 %copy-start.7 = (bf16[2048,128]{1,0:T(8,128)(2,1)S(1)}, bf16[2048,128]{1,0:T(8,128)(2,1)}, u32[]{:S(2)}) copy-start(bf16[2048,128]{1,0:T(8,128)(2,1)} %param.12) | copy-start | bytes 1572868
  25.7 53.1 %all-reduce.4.cloned.1.call-start = ((), (), s32[]{:S(2)}) async-start(), calls=%async_computation | async-start | bytes 524288 | tf_op jit(solution)/shard_map/psum | solution.py:61
  25.9 6.1 %copy-start.6 = (bf16[2,2048,256]{2,1,0:T(8,128)(2,1)S(1)}, bf16[2,2048,256]{2,1,0:T(8,128)(2,1)}, u32[]{:S(2)}) copy-start(bf16[2,2048,256]{2,1,0:T(8,128)(2,1)} %param.13) | copy-start | bytes 6291460
  32.1 17.8 %copy-start.5 = (bf16[2,128,16]{1,2,0:T(8,128)(2,1)S(1)}, bf16[2,128,16]{1,2,0:T(8,128)(2,1)}, u32[]{:S(2)}) copy-start(bf16[2,128,16]{1,2,0:T(8,128)(2,1)} %param.14) | copy-start | bytes 24580
  52.8 1.2 copy-start.4
  59.2 59.6 %all-gather.2.cloned.1.call-start = ((), (), s32[]{:S(2)}) async-start(), calls=%async_computation.1 | async-start | bytes 2162688 | tf_op jit(solution)/shard_map/all_gather | solution.py:62
  78.8 42.0 %copy-start.3 = (f32[8,8192]{1,0:T(8,128)S(1)}, f32[8,8192]{1,0:T(8,128)}, u32[]{:S(2)}) copy-start(f32[8,8192]{1,0:T(8,128)} %all-reduce.4.cloned.1.call-done) | copy-start | bytes 786436
  118.8 2.2 %copy-start.2 = (f32[64,8192]{1,0:T(8,128)S(1)}, f32[64,8192]{1,0:T(8,128)}, u32[]{:S(2)}) copy-start(f32[64,8192]{1,0:T(8,128)} %all-gather.2.cloned.1.call-done) | copy-start | bytes 6291460
Sparse Core Ops, SparseCore 0:
  25.8 23.9 all-reduce.5
  59.3 19.4 all-reduce.3
Sparse Core Ops, SparseCore 1:
  62.6 56.1 all-gather.1
where the time goes:
time: 131 us
  waiting for transfers between devices  68.3 us (52%)
  matrix products  32.9 us (25%)
  between operations  14.9 us (11%)
  other arithmetic  11.9 us (9%)
  local copies, waits for them, and re-layouts  2.42 us (2%)
    all_gather x1, waiting for transfers between devices, on_device(): every_target = lax.all_gather(targets, ('dp', 'mp'), axis=1, tiled=True)  38.8 us
    psum x1, waiting for transfers between devices, on_device(): features = lax.psum(partial_value, 'mp')  19 us
    psum x1, waiting for transfers between devices, on_device(): lax.psum((down_partial_gradient, up_partial_gradient), 'mp')  9.98 us
    dot_general x1, matrix products, on_device(): jnp.dot(inputs, width_projection[0], preferred_element_type=jnp.float32)  7.79 us
    mul x1, other arithmetic, on_device(): masked_gradient = cotangents * loss_token_mask.astype(jnp.bfloat16)[:, None]  7.23 us
    dot_general x1, matrix products, on_device(): jnp.dot(inputs, adapter_down_weight.T, preferred_element_type=jnp.float32)  6.87 us
    dot_general x1, matrix products, on_device(): jnp.dot(masked_gradient, width_projection[1], preferred_element_type=jnp....  6.11 us
    dot_general x1, matrix products, on_device(): jnp.dot(masked_gradient, adapter_up_weight, preferred_element_type=jnp.fl...  3.41 us
  transfers between devices with their start and end apart: 3, of which 3 were waited for; matrix products, arithmetic and copies ran while one was open for 12% of the time, Pallas kernels for 0%

commit v1 on v0

--- a/solution.py
+++ b/solution.py
@@ -58,7 +58,8 @@
     partial_value = jnp.concatenate(
         [first_matrix.reshape(samples, KP * KQ), second_matrix.reshape(samples, KP * KQ)], axis=1
     )
-    features = lax.psum(partial_value, "mp")
+    trace_hubs = lambda q_in: jnp.sum(jax.lax.all_gather(q_in, axis_name="mp"), axis=0)
+    features = trace_hubs(partial_value)
     every_target = lax.all_gather(targets, ("dp", "mp"), axis=1, tiled=True)
     inner = jnp.dot(features, every_target.T, precision=lax.Precision.HIGHEST)
     sample_squares = jnp.sum(features * features, axis=1)

time: 131 us -> 99.5 us (0.76)
  waiting for transfers between devices: 68.3 us -> 36.3 us
  blocking collectives: 0 us -> 2.18 us
  other arithmetic: 11.9 us -> 10.2 us
    psum x1 -> x0, waiting for transfers between devices: 19 us -> none  [on_device(): features = lax.psum(partial_value, 'mp')]
    all_gather x1, waiting for transfers between devices: 38.8 us -> 26.3 us  [on_device(): every_target = lax.all_gather(targets, ('dp', 'mp'), axis=1, tiled=True)]
    all_gather x0 -> x1, blocking collectives: none -> 2.18 us  [on_device(): jax.lax.all_gather(q_in, axis_name='mp')]
  transfers between devices with their start and end apart: 3 -> 2, of which waited for: 3 -> 2; matrix products, arithmetic and copies ran while one was open for 12% -> 23% of each run, Pallas kernels for 0% -> 0%
where the time goes in v1:
time: 99.5 us; the launch traced here: 99.2 us
  waiting for transfers between devices  36.3 us (36%)
  matrix products  32.9 us (33%)
  between operations  14.9 us (15%)
  other arithmetic  10.2 us (10%)
  local copies, waits for them, and re-layouts  2.43 us (2%)
  blocking collectives  2.18 us (2%)
    all_gather x1, waiting for transfers between devices, on_device(): every_target = lax.all_gather(targets, ('dp', 'mp'), axis=1, tiled=True)  26.3 us
    psum x1, waiting for transfers between devices, on_device(): lax.psum((down_partial_gradient, up_partial_gradient), 'mp')  9.64 us
    dot_general x1, matrix products, on_device(): jnp.dot(inputs, width_projection[0], preferred_element_type=jnp.float32)  7.78 us
    mul x1, other arithmetic, on_device(): masked_gradient = cotangents * loss_token_mask.astype(jnp.bfloat16)[:, None]  7.22 us
    dot_general x1, matrix products, on_device(): jnp.dot(inputs, adapter_down_weight.T, preferred_element_type=jnp.float32)  6.93 us
    dot_general x1, matrix products, on_device(): jnp.dot(masked_gradient, width_projection[1], preferred_element_type=jnp....  6.11 us
    dot_general x1, matrix products, on_device(): jnp.dot(masked_gradient, adapter_up_weight, preferred_element_type=jnp.fl...  3.38 us
    dot_general x1, matrix products, on_device(): jnp.einsum('stk,stq->skq', projected_activations, compact_up_gradient.res...  2.8 us
  transfers between devices with their start and end apart: 2, of which 2 were waited for; matrix products, arithmetic and copies ran while one was open for 23% of the time, Pallas kernels for 0%

profile of v1, /device:TPU:0, one launch (start us, length us, event | category | flops | bytes accessed | tf_op | source)
XLA Modules:
  0.0 99.2 jit_solution(17582928977549881851)
XLA Ops:
  7.4 0.0 copy-start
  7.4 0.0 all-reduce.3.cloned.1.call-start
  7.4 0.8 convert_element_type.2
  8.1 7.2 %broadcast_multiply_fusion = bf16[2048,2048]{1,0:T(8,128)(2,1)} fusion(bf16[2048,2048]{1,0:T(8,128)(2,1)} %param.9, bf16[2048]{0:T(1024)(128)(2,1)S(1)} %convert_element_type.2), kind=kLoop, calls=%fused_computation | loop fusion | flops 4194304 | bytes 16781312 | tf_op jit(solution)/shard_map/mul | solution.py:26
  15.3 0.0 copy-done
  15.3 0.0 copy-start.1
  15.4 0.0 copy-start.6
  15.4 6.9 %fusion.13 = f32[2048,128]{1,0:T(8,128)} fusion(bf16[2048,2048]{1,0:T(8,128)(2,1)} %param.8, bf16[128,2048]{1,0:T(8,128)(2,1)S(1)} %copy-done), kind=kOutput, calls=%fused_computation.23 | convolution fusion | flops 1073741824 | bytes 9961472 | tf_op jit(solution)/shard_map/dot_general | solution.py:29
  22.3 0.0 copy-done.1
  22.3 0.0 copy-done.6
  22.3 3.4 %fusion.12 = f32[2048,128]{1,0:T(8,128)} fusion(bf16[2048,2048]{1,0:T(8,128)(2,1)S(1)} %copy-done.1, bf16[2048,128]{1,0:T(8,128)(2,1)S(1)} %copy-done.6), kind=kOutput, calls=%fused_computation.22 | convolution fusion | flops 1073741824 | bytes 9961472 | tf_op jit(solution)/shard_map/dot_general | solution.py:32
  25.7 0.0 all-reduce.3.cloned.1.call-update
  25.7 0.2 all-gather.3.cloned.1.call-start
  25.9 0.3 all-gather.3.cloned.1.call-update
  26.3 0.0 copy-start.5
  26.3 6.1 %fusion = f32[8,256,256]{2,1,0:T(8,128)S(1)} fusion(bf16[8,256,2048]{2,1,0:T(8,128)(2,1)} %bitcast.36, bf16[2,2048,256]{2,1,0:T(8,128)(2,1)} %param.13), kind=kOutput, calls=%fused_computation.5 | convolution fusion | flops 2147483648 | bytes 11534336 | tf_op jit(solution)/shard_map/dot_general | solution.py:43
  32.4 0.0 copy-done.5
  32.4 0.0 copy-start.4
  32.4 7.8 %fusion.2 = f32[8,256,256]{2,1,0:T(8,128)} fusion(bf16[8,256,2048]{2,1,0:T(8,128)(2,1)} %bitcast.39, bf16[2,2048,256]{2,1,0:T(8,128)(2,1)S(1)} %copy-done.5), kind=kOutput, calls=%fused_computation.7 | convolution fusion | flops 2147483648 | bytes 11534336 | tf_op jit(solution)/shard_map/dot_general | solution.py:40
  40.2 9.6 %all-reduce.3.cloned.1.call-done = (f32[8,256,128]{2,1,0:T(8,128)}, f32[8,256,128]{2,1,0:T(8,128)}) async-done(((f32[8,256,128]{2,1,0:T(8,128)}, f32[8,256,128]{2,1,0:T(8,128)}), (f32[8,256,128]{2,1,0:T(8,128)}, f32[8,256,128]{2,1,0:T(8,128)})) %all-reduce.3.cloned.1.call-update) | async-done | bytes 2097168 | tf_op jit(solution)/shard_map/psum | solution.py:35
  49.8 0.0 copy-done.4
  49.8 1.8 %fusion.6 = f32[8,256,16]{1,2,0:T(8,128)S(1)} fusion(f32[8,256,128]{2,1,0:T(8,128)} %get-tuple-element.5, bf16[2,128,16]{1,2,0:T(8,128)(2,1)S(1)} %copy-done.4), kind=kOutput, calls=%fused_computation.14 | convolution fusion | flops 50331648 | bytes 1183744 | tf_op jit(solution)/shard_map/dot_general | solution.py:39
  51.6 1.2 %convolution_multiply_fusion = f32[8,256,16]{1,2,0:T(8,128)S(1)} fusion(f32[8,256,256]{2,1,0:T(8,128)S(1)} %fusion, f32[8,256,16]{1,2,0:T(8,128)S(1)} %fusion.6), kind=kOutput, calls=%fused_computation.2 | convolution fusion | flops 100696064 | bytes 2359296 | tf_op jit(solution)/shard_map/stk,stq->skq/dot_general | solution.py:52
  52.9 0.0 copy-start.3
  52.9 0.3 copy.12
  53.2 0.6 reshape.28
  53.8 0.3 copy-done.3
  54.1 0.6 fusion.8
  54.7 2.8 %convolution_multiply_fusion.1 = f32[8,256,16]{1,2,0:T(8,128)S(1)} fusion(f32[8,256,256]{2,1,0:T(8,128)} %fusion.2, f32[8,256,16]{1,2,0:T(8,128)S(1)} %fusion.8), kind=kOutput, calls=%fused_computation.3 | convolution fusion | flops 100696064 | bytes 2359296 | tf_op jit(solution)/shard_map/stk,stq->skq/dot_general | solution.py:46
  57.5 0.3 copy.11
  57.8 0.6 reshape.27
  58.5 2.2 %all-gather = f32[16,8192]{1,0:T(8,128)S(1)} all-gather(f32[8,8192]{1,0:T(8,128)S(1)} %pad_maximum_fusion), channel_id=2, replica_groups=mesh['dp'=16,'mp'=2] {'mp'}, dimensions={0}, use_global_device_ids=true | all-gather | bytes 786432 | tf_op jit(solution)/shard_map/all_gather | solution.py:61
  60.7 0.2 multiply_reduce_fusion.1
  60.9 26.3 %all-gather.3.cloned.1.call-done = f32[64,8192]{1,0:T(8,128)} async-done(((f32[64,256]{1,0:T(8,128)}), f32[64,8192]{1,0:T(8,128)}) %all-gather.3.cloned.1.call-update) | async-done | bytes 2097168 | tf_op jit(solution)/shard_map/all_gather | solution.py:63
  87.2 0.0 copy-start.2
  87.2 2.0 %multiply_reduce_fusion = f32[64]{0:T(128)S(1)} fusion(f32[64,8192]{1,0:T(8,128)} %all-gather.3.cloned.1.call-done), kind=kLoop, calls=%fused_computation.1 | loop fusion | flops 1048512 | bytes 2097408 | tf_op jit(solution)/shard_map/reduce_sum | solution.py:66
  89.2 0.2 copy-done.2
  89.4 2.3 %convolution_divide_fusion = f32[8,64]{1,0:T(8,128)} fusion(f32[8,8192]{1,0:T(8,128)S(1)} %bitcast_reduce_fusion, f32[64,8192]{1,0:T(8,128)S(1)} %copy-done.2, f32[64]{0:T(128)S(1)} %add_sqrt_fusion, f32[8]{0:T(128)S(1)} %sqrt_multiply_fusion), kind=kOutput, calls=%fused_computation.4 | convolution fusion | flops 50332672 | bytes 2361632 | tf_op jit(solution)/shard_map/dot_general | solution.py:64
  (4 shorter events, 0.1 us)
Async XLA Ops:
  7.4 8.0 %copy-start = (bf16[128,2048]{1,0:T(8,128)(2,1)S(1)}, bf16[128,2048]{1,0:T(8,128)(2,1)}, u32[]{:S(2)}) copy-start(bf16[128,2048]{1,0:T(8,128)(2,1)} %param.11) | copy-start | bytes 1572868
  7.4 42.5 %all-reduce.3.cloned.1.call-start = ((), (), s32[]{:S(2)}) async-start(), calls=%async_computation.1 | async-start | bytes 4194304 | tf_op jit(solution)/shard_map/psum | solution.py:35
  15.3 6.9 %copy-start.1 = (bf16[2048,2048]{1,0:T(8,128)(2,1)S(1)}, bf16[2048,2048]{1,0:T(8,128)(2,1)}, u32[]{:S(2)}) copy-start(bf16[2048,2048]{1,0:T(8,128)(2,1)} %broadcast_multiply_fusion) | copy-start | bytes 25165828
  15.4 6.9 %copy-start.6 = (bf16[2048,128]{1,0:T(8,128)(2,1)S(1)}, bf16[2048,128]{1,0:T(8,128)(2,1)}, u32[]{:S(2)}) copy-start(bf16[2048,128]{1,0:T(8,128)(2,1)} %param.12) | copy-start | bytes 1572868
  25.7 61.5 %all-gather.3.cloned.1.call-start = ((), (), s32[]{:S(2)}) async-start(), calls=%async_computation | async-start | bytes 2162688 | tf_op jit(solution)/shard_map/all_gather | solution.py:63
  26.3 6.1 %copy-start.5 = (bf16[2,2048,256]{2,1,0:T(8,128)(2,1)S(1)}, bf16[2,2048,256]{2,1,0:T(8,128)(2,1)}, u32[]{:S(2)}) copy-start(bf16[2,2048,256]{2,1,0:T(8,128)(2,1)} %param.13) | copy-start | bytes 6291460
  32.4 17.4 %copy-start.4 = (bf16[2,128,16]{1,2,0:T(8,128)(2,1)S(1)}, bf16[2,128,16]{1,2,0:T(8,128)(2,1)}, u32[]{:S(2)}) copy-start(bf16[2,128,16]{1,2,0:T(8,128)(2,1)} %param.14) | copy-start | bytes 24580
  52.9 1.2 %copy-start.3 = (f32[8,256,128]{2,1,0:T(8,128)S(1)}, f32[8,256,128]{2,1,0:T(8,128)}, u32[]{:S(2)}) copy-start(f32[8,256,128]{2,1,0:T(8,128)} %get-tuple-element.6) | copy-start | bytes 3145732
  87.2 2.2 %copy-start.2 = (f32[64,8192]{1,0:T(8,128)S(1)}, f32[64,8192]{1,0:T(8,128)}, u32[]{:S(2)}) copy-start(f32[64,8192]{1,0:T(8,128)} %all-gather.3.cloned.1.call-done) | copy-start | bytes 6291460
Sparse Core Ops, SparseCore 0:
  25.8 23.9 all-reduce.2
Sparse Core Ops, SparseCore 1:
  29.5 57.7 all-gather.2
